TPU v7x, 256 devices: a whole 4x4x8 slice. The times are simulated.
256 devices in a mesh: gy: 8 (over y, core), gx: 32 (over x, z).
Axes of the slice: x: 4, y: 4, z: 8, core: 2. Of those that a mesh axis runs over, the one named last changes fastest.
Arguments:
- phase: float32 [2, 256, 4096], P(None, 'gy', 'gx'), may hold values from -1.5 to 1.5
- velocity: float32 [2, 256, 4096], P(None, 'gy', 'gx'), may hold values from -2 to 2
- offsets: int32 [2, 8], replicated, may hold values from 0 to 4092, as said below
Outputs:
- phase_out: float32 [2, 256, 4096], P(None, 'gy', 'gx')
Inputs may be any that keep to these rules, and one draw needn't show every extreme that they name: `offsets`: every offset is a multiple of 2 ** 2.
All inputs are finite; a program needn't handle non-finite values.
Results may differ from a plain program's by a relative error of at most 0.00014.
Values sent between devices are 32-bit elements; how exact they have to be, the bound alone decides.
A program may use at most 64 MiB of HBM per device.

v0:
```python
import jax
import jax.numpy as jnp
from jax import lax
from jax.experimental import pallas as pl
from jax.experimental.pallas import tpu as pltpu
from jax.sharding import PartitionSpec as P

MESH = pl.DeviceIdType.MESH
NGY, NGX = 8, 32
RELAX, DIFFUSION, REACTION, ADVECTION = 0.8, 4.0, 0.5, 0.5
COUPLING = [DIFFUSION / 4.0**level for level in range(3)]
DIAGONAL = [1.0 + 4.0 * c + 2.0 for c in COUPLING]
SCALE = [RELAX / d for d in DIAGONAL]
COARSE = 4


def lanes(shape=(8, 128)):
    return lax.broadcasted_iota(jnp.int32, shape, len(shape) - 1)


def lane_roll(v, shift):
    return pltpu.roll(v, shift, 1)


def right_of(v):
    last = lane_roll(v[0], 127)[None]
    return last if v.shape[0] == 1 else jnp.concatenate([v[1:], last], axis=0)


def left_of(v):
    first = lane_roll(v[v.shape[0] - 1], 1)[None]
    return first if v.shape[0] == 1 else jnp.concatenate([first, v[:-1]], axis=0)


def sub_roll(v, shift):
    return jnp.stack([pltpu.roll(v[k], shift, 0) for k in range(v.shape[0])])


def vertical(rows):
    count = len(rows)
    after = rows[1:] + [sub_roll(rows[0], 7)]
    before = [sub_roll(rows[count - 1], 1)] + rows[:-1]
    return [a + b for a, b in zip(after, before)]


def beside(rows):
    return [s + (right_of(v) + left_of(v)) for s, v in zip(vertical(rows), rows)]


def coarser(rows):
    out = []
    for r in range(0, len(rows), 2):
        s = rows[r] + rows[r + 1]
        out.append(0.25 * jnp.stack([s[k] + s[k + 1] for k in range(0, s.shape[0], 2)]))
    return out


def finer(rows):
    out = []
    for v in rows:
        wide = jnp.stack([v[k // 2] for k in range(2 * v.shape[0])])
        out += [wide, wide]
    return out


def of_planes(total, difference):
    return jnp.where(lanes() < 64, jnp.float32(total), jnp.float32(difference))


def mixed(v):
    other = jnp.stack([lane_roll(v[k], 64) for k in range(v.shape[0])])
    return jnp.where((lanes() < 64)[None], v + other, other - v)


def operate(rows):
    d = of_planes(DIAGONAL[0] - 2.0, DIAGONAL[0] + 2.0)
    return [d * v - COUPLING[0] * b for v, b in zip(rows, beside(rows))]


def smoothing(level):
    d, s = DIAGONAL[level], SCALE[level]
    return s, of_planes(1.0 - s * (d - 2.0), 1.0 - s * (d + 2.0)), s * COUPLING[level]


def precondition(rows, level=0):
    scale, keep, spread = smoothing(level)
    if level == 2:
        base = [scale * v for v in rows]
        e = base
        for _ in range(COARSE - 1):
            e = [f + keep * v + spread * b for f, v, b in zip(base, e, beside(e))]
        return e
    defect = [keep * v + spread * b for v, b in zip(rows, beside(rows))]
    correction = finer(precondition(coarser(defect), level + 1))
    e = [scale * v + c for v, c in zip(rows, correction)]
    return [scale * f + keep * v + spread * b for f, v, b in zip(rows, e, beside(e))]


def residual_of(u, v):
    out = []
    for s, f, speed in zip(vertical(u), u, v):
        east, west = right_of(f), left_of(f)
        around = s + (east + west)
        source = f + REACTION * (f - f * f * f) - ADVECTION * speed * (east - west)
        other = jnp.stack([lane_roll(f[k], 64) for k in range(4)])
        applied = DIAGONAL[0] * f - COUPLING[0] * around - 2.0 * other
        out.append(mixed(source - applied))
    return out


def own_sum(first, second):
    total = None
    for a, b in zip(first, second):
        product = a * b
        part = (product[0] + product[1]) + (product[2] + product[3])
        total = part if total is None else total + part
    m = lanes() & 63
    total = jnp.where((m >= 16) & (m < 48), total, 0.0)
    return total[3:4] + total[4:5]


def packed_sums(pairs):
    sums = [own_sum(a, b) for a, b in pairs]
    tile = jnp.concatenate(sums + [jnp.zeros((8 - len(sums), 128), jnp.float32)], axis=0)
    for shift in (64, 32, 16):
        tile = tile + lane_roll(tile, shift)
    row = lax.broadcasted_iota(jnp.int32, (8, 128), 0)
    return jnp.sum(jnp.where((lanes() >> 4) == row, tile, 0.0), axis=0, keepdims=True)


def coefficients(packed):
    group = lanes((1, 128)) >> 4
    rw, wq, rz, qz, zy = (
        jnp.sum(jnp.where(group == d, packed, 0.0), axis=1, keepdims=True) for d in range(5)
    )
    a0 = rw / wq
    following = a0 * (a0 * qz - rz)
    b = 1.0 + following / rw
    a1 = following / (b * b * wq - 2.0 * b * a0 * qz + a0 * a0 * zy)
    return a0 + a1 * b, -a1 * a0


def permuted(x, matrix):
    n = x.shape[0]
    high = x.astype(jnp.bfloat16)
    rest = x - high.astype(jnp.float32)
    mid = rest.astype(jnp.bfloat16)
    low = (rest - mid.astype(jnp.float32)).astype(jnp.bfloat16)
    y = jnp.dot(jnp.concatenate([high, mid, low], axis=0), matrix, preferred_element_type=jnp.float32)
    return (y[:n] + y[n : 2 * n]) + y[2 * n :]


def kernel(
    offsets, phase, velocity, out,
    own, got, spread, west, east, sent, later, third, window, ahead, stage,
    own2, got2, west2, east2, window2,
    part, part_row, sums_row, sums_col, part2, part2_row, sums2_row, sums2_col,
    ssem, rsem, s2sem, r2sem,
):
    j, i = lax.axis_index("gy"), lax.axis_index("gx")
    field, pair = i // 16, lax.rem(i, 16)
    up, down = lax.rem(j + 1, NGY), lax.rem(j + NGY - 1, NGY)
    up2, down2 = lax.rem(j + 2, NGY), lax.rem(j + NGY - 2, NGY)
    far = (pair < 4) | (pair >= 12)
    far_row = jnp.where(pair < 4, down2, up2)
    far_slot = field * 64 + jnp.where(pair < 4, 56 + pair, pair - 8)
    near_west, near_east = lax.rem(i + NGX - 1, NGX), lax.rem(i + 1, NGX)

    def tile(ref, slot, count=1):
        return ref.at[pl.ds(pl.multiple_of(slot * 8, 8), 8 * count)]

    def copy(src, dst, ss, rs, row, column):
        return pltpu.make_async_remote_copy(
            src_ref=src, dst_ref=dst, send_sem=ss, recv_sem=rs, device_id=(row, column), device_id_type=MESH
        )

    def to_row(src, dst, ss, rs):
        def body(d, carry):
            q = lax.rem(i + d, NGX)
            copy(tile(src, q), tile(dst, i), ss, rs, j, q).start()
            return carry

        lax.fori_loop(1, NGX, body, 0)
        dst[pl.ds(pl.multiple_of(i * 8, 8), 8), :] = src[pl.ds(pl.multiple_of(i * 8, 8), 8), :]

    def to_sides(src, dst_west, dst_east, sems):
        copy(src, dst_west, ssem.at[sems], rsem.at[sems], j, near_east).start()
        copy(src, dst_east, ssem.at[sems + 1], rsem.at[sems + 1], j, near_west).start()

    def all_tiles(ref, count, ss, rs):
        return copy(ref.at[pl.ds(0, 8 * count)], ref.at[pl.ds(0, 8 * count)], ss, rs, j, near_east)

    def to_spread(src):
        here = src[...]
        following = jnp.concatenate([here[8:], here[:8]], axis=0)
        m = lanes((256, 128)) & 63
        spread[...] = jnp.where(m < 32, here, lane_roll(following, 32))

    def to_windows(dst, variant, shift):
        start = lax.rem(shift // 4 + (4096 - 16), 1024)
        block, g = start // 32, lax.rem(start, 32)
        near = spread[...].reshape(32, 8, 128)
        whole = jnp.full((8, 128), block, jnp.int32)
        for bit in range(5):
            step = 1 << bit
            ahead_of = jnp.concatenate([near[step:], near[:step]], axis=0)
            near = jnp.where(((whole & step) != 0)[None], ahead_of, near)
        next_ = jnp.concatenate([near[2:], near[:2]], axis=0)
        m = lanes((256, 128)) & 63
        near, next_ = near.reshape(256, 128), next_.reshape(256, 128)
        dst[pl.ds(variant * 256, 256), :] = jnp.where(
            m + g < 64, lane_roll(near, lax.rem(128 - g, 128)), lane_roll(next_, 64 - g)
        )

    def shifts(step):
        above, below = offsets[step, up], offsets[step, j]
        second = jnp.where(pair < 4, below + offsets[step, down], -(above + offsets[step, up2]))
        return -above, below, second

    def to_windows_of(dst, step):
        for variant, shift in enumerate(shifts(step)):
            to_windows(dst, variant, shift)

    def to_columns(src, dst, ss, rs):
        def body(n, carry):
            c = lax.rem(i + n, NGX)
            copy(tile(src, c), tile(dst, field * 64 + 8 + pair), ss, rs, up, c).start()
            copy(tile(src, 32 + c), tile(dst, field * 64 + 40 + pair), ss, rs, down, c).start()
            return carry

        lax.fori_loop(0, NGX, body, 0)

        @pl.when(far)
        def _():
            def far_body(n, carry):
                c = lax.rem(i + n, NGX)
                copy(tile(src, 64 + c), tile(dst, far_slot), ss, rs, far_row, c).start()
                return carry

            lax.fori_loop(0, NGX, far_body, 0)

    def columns_sent(src, ss, rs):
        all_tiles(src, 64, ss, rs).wait_send()

        @pl.when(far)
        def _():
            all_tiles(src, 32, ss, rs).wait_send()

    def own_windows(centre, side_west, side_east, targets):
        m = lanes((128, 128)) & 63
        for f in range(2):
            at = pl.ds(128 * f, 128)
            whole = jnp.where(
                m < 16,
                lane_roll(side_west[at, :], 112),
                jnp.where(m < 48, lane_roll(centre[at, :], 16), lane_roll(side_east[at, :], 48)),
            )
            for target in targets:
                target[512 * f + 192 : 512 * f + 320, :] = whole

    def rows_of(ref, f):
        return [
            jnp.stack([ref[pl.ds(512 * f + 4 * r + k, 8, stride=64), :] for k in range(4)])
            for r in range(16)
        ]

    def put_rows(ref, f, rows):
        for r in range(16):
            for k in range(4):
                ref[pl.ds(512 * f + 4 * r + k, 8, stride=64), :] = rows[r][k]

    def sums_to_row(value, mine, dst, sems):
        mine[...] = value
        dst[i] = value

        def body(d, carry):
            q = lax.rem(i + d, NGX)
            copy(mine, dst.at[i], s2sem.at[sems], r2sem.at[sems], j, q).start()
            return carry

        lax.fori_loop(1, NGX, body, 0)

    def sums_to_col(value, mine, dst, sems):
        mine[...] = value
        dst[j] = value

        def body(d, carry):
            q = lax.rem(j + d, NGY)
            copy(mine, dst.at[j], s2sem.at[sems], r2sem.at[sems], q, i).start()
            return carry

        lax.fori_loop(1, NGY, body, 0)

    def few(ref, count, sems):
        return copy(ref.at[pl.ds(0, count)], ref.at[pl.ds(0, count)], s2sem.at[sems], r2sem.at[sems], j, near_east)

    n = lanes((128, 512))
    c = lax.broadcasted_iota(jnp.int32, (128, 512), 0)
    matrix = jnp.where(c == 4 * (n & 127) + (n >> 7), 1.0, 0.0).astype(jnp.bfloat16)
    blocks = jnp.concatenate([phase[0], phase[1], velocity[0], velocity[1]], axis=0)
    split = permuted(blocks, matrix)
    for f in range(2):
        for k in range(4):
            cut = split[64 * f : 64 * f + 64, 128 * k : 128 * k + 128]
            own[pl.ds(128 * f + k, 32, stride=4), :] = cut[:32] + lane_roll(cut[32:], 64)

    to_row(own, got, ssem.at[0], rsem.at[0])
    to_sides(own, west, east, 1)
    for ref in (window, ahead, window2):
        for f in range(2):
            ref[512 * f : 512 * f + 32, :] = jnp.zeros((32, 128), jnp.float32)
            ref[512 * f + 480 : 512 * f + 512, :] = jnp.zeros((32, 128), jnp.float32)
    all_tiles(got, 31, ssem.at[0], rsem.at[0]).wait_recv()
    to_spread(got)
    to_windows_of(sent, 0)
    to_columns(sent, window, ssem.at[3], rsem.at[3])
    to_windows_of(later, 1)
    to_columns(later, ahead, ssem.at[4], rsem.at[4])
    all_tiles(west, 32, ssem.at[1], rsem.at[1]).wait_recv()
    all_tiles(east, 32, ssem.at[2], rsem.at[2]).wait_recv()
    own_windows(own, west, east, (window, ahead))
    all_tiles(window, 80, ssem.at[3], rsem.at[3]).wait_recv()

    def solve(u, v):
        r = residual_of(u, v)
        w = precondition(r)
        q = operate(w)
        z = precondition(q)
        y = operate(z)
        return w, z, packed_sums(((r, w), (w, q), (r, z), (q, z), (z, y)))

    w, z, packed = solve(rows_of(window, 0), rows_of(window, 1))
    put_rows(stage, 0, w)
    put_rows(stage, 1, z)
    for f in range(2):
        own2[128 * f : 128 * f + 128, :] = lane_roll(stage[512 * f + 192 : 512 * f + 320, :], 112)
    to_row(own2, got2, ssem.at[5], rsem.at[5])
    sums_to_row(packed, part, sums_row, 0)
    to_sides(own2, west2, east2, 6)
    all_tiles(got2, 31, ssem.at[5], rsem.at[5]).wait_recv()
    to_spread(got2)
    to_windows_of(third, 1)
    to_columns(third, window2, ssem.at[8], rsem.at[8])
    few(sums_row, 31, 0).wait_recv()
    sums_to_col(jnp.sum(sums_row[...], axis=0), part_row, sums_col, 1)
    all_tiles(west2, 32, ssem.at[6], rsem.at[6]).wait_recv()
    all_tiles(east2, 32, ssem.at[7], rsem.at[7]).wait_recv()
    own_windows(own2, west2, east2, (window2,))
    few(sums_col, 7, 1).wait_recv()
    c1, c2 = coefficients(jnp.sum(sums_col[...], axis=0))
    all_tiles(ahead, 80, ssem.at[4], rsem.at[4]).wait_recv()
    all_tiles(window2, 80, ssem.at[8], rsem.at[8]).wait_recv()

    def moved(u, w, z, c1, c2):
        return [a + 0.5 * mixed(c1 * b + c2 * d) for a, b, d in zip(u, w, z)]

    u = moved(rows_of(ahead, 0), rows_of(window2, 0), rows_of(window2, 1), c1, c2)
    w, z, packed = solve(u, rows_of(ahead, 1))
    sums_to_row(packed, part2, sums2_row, 2)
    few(sums2_row, 31, 2).wait_recv()
    sums_to_col(jnp.sum(sums2_row[...], axis=0), part2_row, sums2_col, 3)
    few(sums2_col, 7, 3).wait_recv()
    c1, c2 = coefficients(jnp.sum(sums2_col[...], axis=0))
    put_rows(stage, 0, moved(u, w, z, c1, c2))
    flat = jnp.concatenate([stage[pl.ds(192 + k, 32, stride=4), :] for k in range(4)], axis=1)
    rho = lax.broadcasted_iota(jnp.int32, (512, 256), 0)
    col = lanes((512, 256))
    c = col & 127
    back = ((rho >> 7) == (c & 3)) & ((rho & 127) == (col >> 7) * 64 + 16 + (c >> 2))
    flat = permuted(flat, jnp.where(back, 1.0, 0.0).astype(jnp.bfloat16))
    out[0] = flat[:, :128]
    out[1] = flat[:, 128:]

    all_tiles(own, 31, ssem.at[0], rsem.at[0]).wait_send()
    all_tiles(own, 32, ssem.at[1], rsem.at[1]).wait_send()
    all_tiles(own, 32, ssem.at[2], rsem.at[2]).wait_send()
    columns_sent(sent, ssem.at[3], rsem.at[3])
    columns_sent(later, ssem.at[4], rsem.at[4])
    all_tiles(own2, 31, ssem.at[5], rsem.at[5]).wait_send()
    all_tiles(own2, 32, ssem.at[6], rsem.at[6]).wait_send()
    all_tiles(own2, 32, ssem.at[7], rsem.at[7]).wait_send()
    columns_sent(third, ssem.at[8], rsem.at[8])
    few(sums_row, 31, 0).wait_send()
    few(sums_col, 7, 1).wait_send()
    few(sums2_row, 31, 2).wait_send()
    few(sums2_col, 7, 3).wait_send()


def local(phase, velocity, offsets):
    f32 = jnp.float32
    tiles = lambda count: pltpu.VMEM((8 * count, 128), f32)
    line, lines = pltpu.VMEM((1, 128), f32), lambda n: pltpu.VMEM((n, 1, 128), f32)
    vmem = pl.BlockSpec(memory_space=pltpu.VMEM)
    return pl.pallas_call(
        kernel,
        out_shape=jax.ShapeDtypeStruct(phase.shape, f32),
        in_specs=[pl.BlockSpec(memory_space=pltpu.SMEM), vmem, vmem],
        out_specs=vmem,
        scratch_shapes=[
            tiles(32), tiles(32), tiles(32), tiles(32), tiles(32), tiles(96), tiles(96), tiles(96), tiles(128), tiles(128), tiles(128),
            tiles(32), tiles(32), tiles(32), tiles(32), tiles(128),
            line, line, lines(32), lines(8), line, line, lines(32), lines(8),
            pltpu.SemaphoreType.DMA((9,)), pltpu.SemaphoreType.DMA((9,)),
            pltpu.SemaphoreType.DMA((4,)), pltpu.SemaphoreType.DMA((4,)),
        ],
        compiler_params=pltpu.CompilerParams(has_side_effects=True),
    )(offsets, phase, velocity)


def solution(mesh):
    return jax.shard_map(
        local,
        mesh=mesh,
        in_specs=(P(None, "gy", "gx"), P(None, "gy", "gx"), P()),
        out_specs=P(None, "gy", "gx"),
        check_vma=False,
    )
```

profile of v0, /device:TPU:1, one launch (start us, length us, event | category | flops | bytes accessed | tf_op | source)
XLA Modules:
  0.0 76.4 jit_solution(6804525552854742291)
XLA Ops:
  0.0 75.0 %shard_map.37 = f32[2,32,128]{2,1,0:T(8,128)} custom-call(s32[2,8]{1,0:T(2,128)} %offsets.1, f32[2,32,128]{2,1,0:T(8,128)} %phase.1, f32[2,32,128]{2,1,0:T(8,128)} %velocity.1), custom_call_target="tpu_custom_call" | custom-call | tf_op jit(solution)/shard_map/pallas_call | solution.py:394
  75.0 1.4 %copy.5 = f32[2,32,128]{2,1,0:T(8,128)} copy(f32[2,32,128]{2,1,0:T(8,128)} %shard_map.37) | data formatting | bytes 65536
where the time goes:
time: 76.6 us; the launch traced here: 76.4 us
  Pallas kernels  75 us (98%)
  local copies, waits for them, and re-layouts  1.38 us (2%)
    pallas_call x1, Pallas kernels, local(): pl.pallas_call(kernel, out_shape=jax.ShapeDtypeStruct(phase.shape, f32),...  75 us

commit v1 on v0

--- a/solution.py
+++ b/solution.py
@@ -155,7 +155,7 @@
     own, got, spread, west, east, sent, later, third, window, ahead, stage,
     own2, got2, west2, east2, window2,
     part, part_row, sums_row, sums_col, part2, part2_row, sums2_row, sums2_col,
-    ssem, rsem, s2sem, r2sem,
+    ssem, rsem, s2sem, r2sem, ready,
 ):
     j, i = lax.axis_index("gy"), lax.axis_index("gx")
     field, pair = i // 16, lax.rem(i, 16)
@@ -294,6 +294,18 @@
     def few(ref, count, sems):
         return copy(ref.at[pl.ds(0, count)], ref.at[pl.ds(0, count)], s2sem.at[sems], r2sem.at[sems], j, near_east)
 
+    pending = []
+
+    barrier = pltpu.get_barrier_semaphore()
+
+    def greet_row(d, carry):
+        pl.semaphore_signal(barrier, inc=1, device_id=(j, lax.rem(i + d, NGX)), device_id_type=MESH)
+        return carry
+
+    lax.fori_loop(1, NGX, greet_row, 0)
+    for d in range(1, NGY):
+        pl.semaphore_signal(barrier, inc=1, device_id=(lax.rem(j + d, NGY), i), device_id_type=MESH)
+
     n = lanes((128, 512))
     c = lax.broadcasted_iota(jnp.int32, (128, 512), 0)
     matrix = jnp.where(c == 4 * (n & 127) + (n >> 7), 1.0, 0.0).astype(jnp.bfloat16)
@@ -304,8 +316,14 @@
             cut = split[64 * f : 64 * f + 64, 128 * k : 128 * k + 128]
             own[pl.ds(128 * f + k, 32, stride=4), :] = cut[:32] + lane_roll(cut[32:], 64)
 
+    pl.semaphore_wait(barrier, NGX - 1 + NGY - 1)
     to_row(own, got, ssem.at[0], rsem.at[0])
+    for row in (up, down, up2, down2):
+        pl.semaphore_signal(ready, inc=1, device_id=(row, i), device_id_type=MESH)
+    pending.append(all_tiles(own, 31, ssem.at[0], rsem.at[0]).wait_send)
     to_sides(own, west, east, 1)
+    pending.append(all_tiles(own, 32, ssem.at[1], rsem.at[1]).wait_send)
+    pending.append(all_tiles(own, 32, ssem.at[2], rsem.at[2]).wait_send)
     for ref in (window, ahead, window2):
         for f in range(2):
             ref[512 * f : 512 * f + 32, :] = jnp.zeros((32, 128), jnp.float32)
@@ -313,9 +331,12 @@
     all_tiles(got, 31, ssem.at[0], rsem.at[0]).wait_recv()
     to_spread(got)
     to_windows_of(sent, 0)
+    pl.semaphore_wait(ready, 4)
     to_columns(sent, window, ssem.at[3], rsem.at[3])
+    pending.append(lambda: columns_sent(sent, ssem.at[3], rsem.at[3]))
     to_windows_of(later, 1)
     to_columns(later, ahead, ssem.at[4], rsem.at[4])
+    pending.append(lambda: columns_sent(later, ssem.at[4], rsem.at[4]))
     all_tiles(west, 32, ssem.at[1], rsem.at[1]).wait_recv()
     all_tiles(east, 32, ssem.at[2], rsem.at[2]).wait_recv()
     own_windows(own, west, east, (window, ahead))
@@ -335,14 +356,20 @@
     for f in range(2):
         own2[128 * f : 128 * f + 128, :] = lane_roll(stage[512 * f + 192 : 512 * f + 320, :], 112)
     to_row(own2, got2, ssem.at[5], rsem.at[5])
+    pending.append(all_tiles(own2, 31, ssem.at[5], rsem.at[5]).wait_send)
     sums_to_row(packed, part, sums_row, 0)
+    pending.append(few(sums_row, 31, 0).wait_send)
     to_sides(own2, west2, east2, 6)
+    pending.append(all_tiles(own2, 32, ssem.at[6], rsem.at[6]).wait_send)
+    pending.append(all_tiles(own2, 32, ssem.at[7], rsem.at[7]).wait_send)
     all_tiles(got2, 31, ssem.at[5], rsem.at[5]).wait_recv()
     to_spread(got2)
     to_windows_of(third, 1)
     to_columns(third, window2, ssem.at[8], rsem.at[8])
+    pending.append(lambda: columns_sent(third, ssem.at[8], rsem.at[8]))
     few(sums_row, 31, 0).wait_recv()
     sums_to_col(jnp.sum(sums_row[...], axis=0), part_row, sums_col, 1)
+    pending.append(few(sums_col, 7, 1).wait_send)
     all_tiles(west2, 32, ssem.at[6], rsem.at[6]).wait_recv()
     all_tiles(east2, 32, ssem.at[7], rsem.at[7]).wait_recv()
     own_windows(own2, west2, east2, (window2,))
@@ -357,8 +384,10 @@
     u = moved(rows_of(ahead, 0), rows_of(window2, 0), rows_of(window2, 1), c1, c2)
     w, z, packed = solve(u, rows_of(ahead, 1))
     sums_to_row(packed, part2, sums2_row, 2)
+    pending.append(few(sums2_row, 31, 2).wait_send)
     few(sums2_row, 31, 2).wait_recv()
     sums_to_col(jnp.sum(sums2_row[...], axis=0), part2_row, sums2_col, 3)
+    pending.append(few(sums2_col, 7, 3).wait_send)
     few(sums2_col, 7, 3).wait_recv()
     c1, c2 = coefficients(jnp.sum(sums2_col[...], axis=0))
     put_rows(stage, 0, moved(u, w, z, c1, c2))
@@ -371,19 +400,8 @@
     out[0] = flat[:, :128]
     out[1] = flat[:, 128:]
 
-    all_tiles(own, 31, ssem.at[0], rsem.at[0]).wait_send()
-    all_tiles(own, 32, ssem.at[1], rsem.at[1]).wait_send()
-    all_tiles(own, 32, ssem.at[2], rsem.at[2]).wait_send()
-    columns_sent(sent, ssem.at[3], rsem.at[3])
-    columns_sent(later, ssem.at[4], rsem.at[4])
-    all_tiles(own2, 31, ssem.at[5], rsem.at[5]).wait_send()
-    all_tiles(own2, 32, ssem.at[6], rsem.at[6]).wait_send()
-    all_tiles(own2, 32, ssem.at[7], rsem.at[7]).wait_send()
-    columns_sent(third, ssem.at[8], rsem.at[8])
-    few(sums_row, 31, 0).wait_send()
-    few(sums_col, 7, 1).wait_send()
-    few(sums2_row, 31, 2).wait_send()
-    few(sums2_col, 7, 3).wait_send()
+    for wait in pending:
+        wait()
 
 
 def local(phase, velocity, offsets):
@@ -401,9 +419,9 @@
             tiles(32), tiles(32), tiles(32), tiles(32), tiles(128),
             line, line, lines(32), lines(8), line, line, lines(32), lines(8),
             pltpu.SemaphoreType.DMA((9,)), pltpu.SemaphoreType.DMA((9,)),
-            pltpu.SemaphoreType.DMA((4,)), pltpu.SemaphoreType.DMA((4,)),
+            pltpu.SemaphoreType.DMA((4,)), pltpu.SemaphoreType.DMA((4,)), pltpu.SemaphoreType.REGULAR,
         ],
-        compiler_params=pltpu.CompilerParams(has_side_effects=True),
+        compiler_params=pltpu.CompilerParams(collective_id=0, has_side_effects=True),
     )(offsets, phase, velocity)
 
 

time: 76.6 us -> 68.4 us (0.89)
  Pallas kernels: 75 us -> 66.8 us
    pallas_call x1, Pallas kernels: 75 us -> 66.8 us  [local(): pl.pallas_call(kernel, out_shape=jax.ShapeDtypeStruct(phase.shape, f32),...]
where the time goes in v1:
time: 68.4 us; the launch traced here: 68.2 us
  Pallas kernels  66.8 us (98%)
  local copies, waits for them, and re-layouts  1.38 us (2%)
    pallas_call x1, Pallas kernels, local(): pl.pallas_call(kernel, out_shape=jax.ShapeDtypeStruct(phase.shape, f32),...  66.8 us
    unnamed x1, local copies, waits for them, and re-layouts  1.38 us

profile of v1, /device:TPU:1, one launch (start us, length us, event | category | flops | bytes accessed | tf_op | source)
XLA Modules:
  0.0 68.2 jit_solution(2141209973036560751)
XLA Ops:
  0.0 66.8 %shard_map.37 = f32[2,32,128]{2,1,0:T(8,128)} custom-call(s32[2,8]{1,0:T(2,128)} %offsets.1, f32[2,32,128]{2,1,0:T(8,128)} %phase.1, f32[2,32,128]{2,1,0:T(8,128)} %velocity.1), custom_call_target="tpu_custom_call" | custom-call | tf_op jit(solution)/shard_map/pallas_call | solution.py:412
  66.8 1.4 %copy.5 = f32[2,32,128]{2,1,0:T(8,128)} copy(f32[2,32,128]{2,1,0:T(8,128)} %shard_map.37) | data formatting | bytes 65536

commit v2 on v1

--- a/solution.py
+++ b/solution.py
@@ -150,20 +150,25 @@
     return (y[:n] + y[n : 2 * n]) + y[2 * n :]
 
 
+def held_by(device):
+    return lax.rem(device, 4) * 4 + device // 8
+
+
 def kernel(
     offsets, phase, velocity, out,
     own, got, spread, west, east, sent, later, third, window, ahead, stage,
-    own2, got2, west2, east2, window2,
+    own2, got2, west2, east2, window2, flat_rows,
     part, part_row, sums_row, sums_col, part2, part2_row, sums2_row, sums2_col,
     ssem, rsem, s2sem, r2sem, ready,
 ):
     j, i = lax.axis_index("gy"), lax.axis_index("gx")
-    field, pair = i // 16, lax.rem(i, 16)
+    chip_x, chip_z = i // 8, lax.rem(i, 8)
+    pair = held_by(i)
     up, down = lax.rem(j + 1, NGY), lax.rem(j + NGY - 1, NGY)
     up2, down2 = lax.rem(j + 2, NGY), lax.rem(j + NGY - 2, NGY)
     far = (pair < 4) | (pair >= 12)
     far_row = jnp.where(pair < 4, down2, up2)
-    far_slot = field * 64 + jnp.where(pair < 4, 56 + pair, pair - 8)
+    far_slot = jnp.where(pair < 4, 56 + pair, pair - 8)
     near_west, near_east = lax.rem(i + NGX - 1, NGX), lax.rem(i + 1, NGX)
 
     def tile(ref, slot, count=1):
@@ -177,11 +182,11 @@
     def to_row(src, dst, ss, rs):
         def body(d, carry):
             q = lax.rem(i + d, NGX)
-            copy(tile(src, q), tile(dst, i), ss, rs, j, q).start()
+            copy(tile(src, held_by(q)), tile(dst, i), ss, rs, j, q).start()
             return carry
 
         lax.fori_loop(1, NGX, body, 0)
-        dst[pl.ds(pl.multiple_of(i * 8, 8), 8), :] = src[pl.ds(pl.multiple_of(i * 8, 8), 8), :]
+        dst[pl.ds(pl.multiple_of(i * 8, 8), 8), :] = src[pl.ds(pl.multiple_of(pair * 8, 8), 8), :]
 
     def to_sides(src, dst_west, dst_east, sems):
         copy(src, dst_west, ssem.at[sems], rsem.at[sems], j, near_east).start()
@@ -194,23 +199,28 @@
         here = src[...]
         following = jnp.concatenate([here[8:], here[:8]], axis=0)
         m = lanes((256, 128)) & 63
-        spread[...] = jnp.where(m < 32, here, lane_roll(following, 32))
+        spread[0:256, :] = jnp.where(m < 32, here, lane_roll(following, 32))
+        spread[256:512, :] = jnp.where(m < 32, lane_roll(here, 96), following)
 
     def to_windows(dst, variant, shift):
         start = lax.rem(shift // 4 + (4096 - 16), 1024)
         block, g = start // 32, lax.rem(start, 32)
-        near = spread[...].reshape(32, 8, 128)
         whole = jnp.full((8, 128), block, jnp.int32)
-        for bit in range(5):
-            step = 1 << bit
-            ahead_of = jnp.concatenate([near[step:], near[:step]], axis=0)
-            near = jnp.where(((whole & step) != 0)[None], ahead_of, near)
-        next_ = jnp.concatenate([near[2:], near[:2]], axis=0)
         m = lanes((256, 128)) & 63
-        near, next_ = near.reshape(256, 128), next_.reshape(256, 128)
-        dst[pl.ds(variant * 256, 256), :] = jnp.where(
-            m + g < 64, lane_roll(near, lax.rem(128 - g, 128)), lane_roll(next_, 64 - g)
-        )
+        for f in range(2):
+            near = spread[256 * f : 256 * f + 256, :].reshape(32, 8, 128)
+            for bit in range(5):
+                step = 1 << bit
+                ahead_of = jnp.concatenate([near[step:], near[:step]], axis=0)
+                near = jnp.where(((whole & step) != 0)[None], ahead_of, near)
+            next_ = jnp.concatenate([near[2:], near[:2]], axis=0)
+            near, next_ = near.reshape(256, 128), next_.reshape(256, 128)
+            moved_on = jnp.where(
+                m + g < 64, lane_roll(near, lax.rem(128 - g, 128)), lane_roll(next_, 64 - g)
+            )
+            for c in range(NGX):
+                at = 16 * (32 * variant + c) + 8 * f
+                dst[at : at + 8, :] = moved_on[8 * c : 8 * c + 8]
 
     def shifts(step):
         above, below = offsets[step, up], offsets[step, j]
@@ -221,23 +231,29 @@
         for variant, shift in enumerate(shifts(step)):
             to_windows(dst, variant, shift)
 
+    def both_fields(ref, slot, count=1):
+        return ref.at[pl.ds(pl.multiple_of(slot * 16, 16), 16 * count)]
+
     def to_columns(src, dst, ss, rs):
+        def served(n):
+            return lax.rem(chip_x + n // 4, 4) * 8 + lax.rem(chip_z + 6 + lax.rem(n, 4), 8)
+
         def body(n, carry):
-            c = lax.rem(i + n, NGX)
-            copy(tile(src, c), tile(dst, field * 64 + 8 + pair), ss, rs, up, c).start()
-            copy(tile(src, 32 + c), tile(dst, field * 64 + 40 + pair), ss, rs, down, c).start()
+            c = served(n)
+            copy(both_fields(src, c), both_fields(dst, 8 + pair), ss, rs, up, c).start()
+            copy(both_fields(src, 32 + c), both_fields(dst, 40 + pair), ss, rs, down, c).start()
             return carry
 
-        lax.fori_loop(0, NGX, body, 0)
+        lax.fori_loop(0, 16, body, 0)
 
         @pl.when(far)
         def _():
             def far_body(n, carry):
-                c = lax.rem(i + n, NGX)
-                copy(tile(src, 64 + c), tile(dst, far_slot), ss, rs, far_row, c).start()
+                c = served(n)
+                copy(both_fields(src, 64 + c), both_fields(dst, far_slot), ss, rs, far_row, c).start()
                 return carry
 
-            lax.fori_loop(0, NGX, far_body, 0)
+            lax.fori_loop(0, 16, far_body, 0)
 
     def columns_sent(src, ss, rs):
         all_tiles(src, 64, ss, rs).wait_send()
@@ -248,26 +264,27 @@
 
     def own_windows(centre, side_west, side_east, targets):
         m = lanes((128, 128)) & 63
-        for f in range(2):
-            at = pl.ds(128 * f, 128)
+        for f, turns in enumerate(((112, 16, 48), (80, 112, 16))):
             whole = jnp.where(
                 m < 16,
-                lane_roll(side_west[at, :], 112),
-                jnp.where(m < 48, lane_roll(centre[at, :], 16), lane_roll(side_east[at, :], 48)),
+                lane_roll(side_west[...], turns[0]),
+                jnp.where(m < 48, lane_roll(centre[...], turns[1]), lane_roll(side_east[...], turns[2])),
             )
             for target in targets:
-                target[512 * f + 192 : 512 * f + 320, :] = whole
+                for p in range(16):
+                    at = 16 * (24 + p) + 8 * f
+                    target[at : at + 8, :] = whole[8 * p : 8 * p + 8]
+
+    def row_at(f, r, k):
+        return pl.ds(16 * (r // 2) + 8 * f + 4 * (r % 2) + k, 8, stride=128)
 
     def rows_of(ref, f):
-        return [
-            jnp.stack([ref[pl.ds(512 * f + 4 * r + k, 8, stride=64), :] for k in range(4)])
-            for r in range(16)
-        ]
+        return [jnp.stack([ref[row_at(f, r, k), :] for k in range(4)]) for r in range(16)]
 
     def put_rows(ref, f, rows):
         for r in range(16):
             for k in range(4):
-                ref[pl.ds(512 * f + 4 * r + k, 8, stride=64), :] = rows[r][k]
+                ref[row_at(f, r, k), :] = rows[r][k]
 
     def sums_to_row(value, mine, dst, sems):
         mine[...] = value
@@ -311,23 +328,22 @@
     matrix = jnp.where(c == 4 * (n & 127) + (n >> 7), 1.0, 0.0).astype(jnp.bfloat16)
     blocks = jnp.concatenate([phase[0], phase[1], velocity[0], velocity[1]], axis=0)
     split = permuted(blocks, matrix)
-    for f in range(2):
-        for k in range(4):
-            cut = split[64 * f : 64 * f + 64, 128 * k : 128 * k + 128]
-            own[pl.ds(128 * f + k, 32, stride=4), :] = cut[:32] + lane_roll(cut[32:], 64)
+    for k in range(4):
+        u, v = (split[64 * f : 64 * f + 64, 128 * k : 128 * k + 128] for f in range(2))
+        u, v = (cut[:32] + lane_roll(cut[32:], 64) for cut in (u, v))
+        own[pl.ds(k, 32, stride=4), :] = u + lane_roll(v, 32)
 
     pl.semaphore_wait(barrier, NGX - 1 + NGY - 1)
     to_row(own, got, ssem.at[0], rsem.at[0])
     for row in (up, down, up2, down2):
         pl.semaphore_signal(ready, inc=1, device_id=(row, i), device_id_type=MESH)
-    pending.append(all_tiles(own, 31, ssem.at[0], rsem.at[0]).wait_send)
+    pending.append(all_tiles(got, 31, ssem.at[0], rsem.at[0]).wait_send)
     to_sides(own, west, east, 1)
-    pending.append(all_tiles(own, 32, ssem.at[1], rsem.at[1]).wait_send)
-    pending.append(all_tiles(own, 32, ssem.at[2], rsem.at[2]).wait_send)
+    pending.append(all_tiles(own, 16, ssem.at[1], rsem.at[1]).wait_send)
+    pending.append(all_tiles(own, 16, ssem.at[2], rsem.at[2]).wait_send)
     for ref in (window, ahead, window2):
-        for f in range(2):
-            ref[512 * f : 512 * f + 32, :] = jnp.zeros((32, 128), jnp.float32)
-            ref[512 * f + 480 : 512 * f + 512, :] = jnp.zeros((32, 128), jnp.float32)
+        ref[0:64, :] = jnp.zeros((64, 128), jnp.float32)
+        ref[960:1024, :] = jnp.zeros((64, 128), jnp.float32)
     all_tiles(got, 31, ssem.at[0], rsem.at[0]).wait_recv()
     to_spread(got)
     to_windows_of(sent, 0)
@@ -337,8 +353,8 @@
     to_windows_of(later, 1)
     to_columns(later, ahead, ssem.at[4], rsem.at[4])
     pending.append(lambda: columns_sent(later, ssem.at[4], rsem.at[4]))
-    all_tiles(west, 32, ssem.at[1], rsem.at[1]).wait_recv()
-    all_tiles(east, 32, ssem.at[2], rsem.at[2]).wait_recv()
+    all_tiles(west, 16, ssem.at[1], rsem.at[1]).wait_recv()
+    all_tiles(east, 16, ssem.at[2], rsem.at[2]).wait_recv()
     own_windows(own, west, east, (window, ahead))
     all_tiles(window, 80, ssem.at[3], rsem.at[3]).wait_recv()
 
@@ -353,15 +369,19 @@
     w, z, packed = solve(rows_of(window, 0), rows_of(window, 1))
     put_rows(stage, 0, w)
     put_rows(stage, 1, z)
-    for f in range(2):
-        own2[128 * f : 128 * f + 128, :] = lane_roll(stage[512 * f + 192 : 512 * f + 320, :], 112)
+    m = lanes() & 63
+    for p in range(16):
+        at = 16 * (24 + p)
+        own2[8 * p : 8 * p + 8, :] = jnp.where(
+            m < 32, lane_roll(stage[at : at + 8, :], 112), lane_roll(stage[at + 8 : at + 16, :], 16)
+        )
     to_row(own2, got2, ssem.at[5], rsem.at[5])
-    pending.append(all_tiles(own2, 31, ssem.at[5], rsem.at[5]).wait_send)
+    pending.append(all_tiles(got2, 31, ssem.at[5], rsem.at[5]).wait_send)
     sums_to_row(packed, part, sums_row, 0)
     pending.append(few(sums_row, 31, 0).wait_send)
     to_sides(own2, west2, east2, 6)
-    pending.append(all_tiles(own2, 32, ssem.at[6], rsem.at[6]).wait_send)
-    pending.append(all_tiles(own2, 32, ssem.at[7], rsem.at[7]).wait_send)
+    pending.append(all_tiles(own2, 16, ssem.at[6], rsem.at[6]).wait_send)
+    pending.append(all_tiles(own2, 16, ssem.at[7], rsem.at[7]).wait_send)
     all_tiles(got2, 31, ssem.at[5], rsem.at[5]).wait_recv()
     to_spread(got2)
     to_windows_of(third, 1)
@@ -370,8 +390,8 @@
     few(sums_row, 31, 0).wait_recv()
     sums_to_col(jnp.sum(sums_row[...], axis=0), part_row, sums_col, 1)
     pending.append(few(sums_col, 7, 1).wait_send)
-    all_tiles(west2, 32, ssem.at[6], rsem.at[6]).wait_recv()
-    all_tiles(east2, 32, ssem.at[7], rsem.at[7]).wait_recv()
+    all_tiles(west2, 16, ssem.at[6], rsem.at[6]).wait_recv()
+    all_tiles(east2, 16, ssem.at[7], rsem.at[7]).wait_recv()
     own_windows(own2, west2, east2, (window2,))
     few(sums_col, 7, 1).wait_recv()
     c1, c2 = coefficients(jnp.sum(sums_col[...], axis=0))
@@ -391,7 +411,9 @@
     few(sums2_col, 7, 3).wait_recv()
     c1, c2 = coefficients(jnp.sum(sums2_col[...], axis=0))
     put_rows(stage, 0, moved(u, w, z, c1, c2))
-    flat = jnp.concatenate([stage[pl.ds(192 + k, 32, stride=4), :] for k in range(4)], axis=1)
+    block = [stage[16 * (24 + p) : 16 * (24 + p) + 8, :] for p in range(16)]
+    flat_rows[...] = jnp.concatenate(block, axis=0)
+    flat = jnp.concatenate([flat_rows[pl.ds(k, 32, stride=4), :] for k in range(4)], axis=1)
     rho = lax.broadcasted_iota(jnp.int32, (512, 256), 0)
     col = lanes((512, 256))
     c = col & 127
@@ -415,8 +437,8 @@
         in_specs=[pl.BlockSpec(memory_space=pltpu.SMEM), vmem, vmem],
         out_specs=vmem,
         scratch_shapes=[
-            tiles(32), tiles(32), tiles(32), tiles(32), tiles(32), tiles(96), tiles(96), tiles(96), tiles(128), tiles(128), tiles(128),
-            tiles(32), tiles(32), tiles(32), tiles(32), tiles(128),
+            tiles(16), tiles(32), tiles(64), tiles(16), tiles(16), tiles(192), tiles(192), tiles(192), tiles(128), tiles(128), tiles(128),
+            tiles(16), tiles(32), tiles(16), tiles(16), tiles(128), tiles(16),
             line, line, lines(32), lines(8), line, line, lines(32), lines(8),
             pltpu.SemaphoreType.DMA((9,)), pltpu.SemaphoreType.DMA((9,)),
             pltpu.SemaphoreType.DMA((4,)), pltpu.SemaphoreType.DMA((4,)), pltpu.SemaphoreType.REGULAR,

time: 68.4 us -> 61.7 us (0.902)
  Pallas kernels: 66.8 us -> 60.1 us
    pallas_call x1, Pallas kernels: 66.8 us -> 60.1 us  [local(): pl.pallas_call(kernel, out_shape=jax.ShapeDtypeStruct(phase.shape, f32),...]
where the time goes in v2:
time: 61.7 us; the launch traced here: 61.5 us
  Pallas kernels  60.1 us (97%)
  local copies, waits for them, and re-layouts  1.38 us (2%)
    pallas_call x1, Pallas kernels, local(): pl.pallas_call(kernel, out_shape=jax.ShapeDtypeStruct(phase.shape, f32),...  60.1 us
    unnamed x1, local copies, waits for them, and re-layouts  1.38 us

profile of v2, /device:TPU:1, one launch (start us, length us, event | category | flops | bytes accessed | tf_op | source)
XLA Modules:
  0.0 61.5 jit_solution(7506454334907676724)
XLA Ops:
  0.0 60.1 %shard_map.37 = f32[2,32,128]{2,1,0:T(8,128)} custom-call(s32[2,8]{1,0:T(2,128)} %offsets.1, f32[2,32,128]{2,1,0:T(8,128)} %phase.1, f32[2,32,128]{2,1,0:T(8,128)} %velocity.1), custom_call_target="tpu_custom_call" | custom-call | tf_op jit(solution)/shard_map/pallas_call | solution.py:434
  60.1 1.4 %copy.5 = f32[2,32,128]{2,1,0:T(8,128)} copy(f32[2,32,128]{2,1,0:T(8,128)} %shard_map.37) | data formatting | bytes 65536

commit v3 on v2

--- a/solution.py
+++ b/solution.py
@@ -158,7 +158,7 @@
     offsets, phase, velocity, out,
     own, got, spread, west, east, sent, later, third, window, ahead, stage,
     own2, got2, west2, east2, window2, flat_rows,
-    part, part_row, sums_row, sums_col, part2, part2_row, sums2_row, sums2_col,
+    part, part_row, sums_row, sums_col, part2, part2_chip, sums2_core, sums2,
     ssem, rsem, s2sem, r2sem, ready,
 ):
     j, i = lax.axis_index("gy"), lax.axis_index("gx")
@@ -227,33 +227,26 @@
         second = jnp.where(pair < 4, below + offsets[step, down], -(above + offsets[step, up2]))
         return -above, below, second
 
-    def to_windows_of(dst, step):
-        for variant, shift in enumerate(shifts(step)):
-            to_windows(dst, variant, shift)
-
     def both_fields(ref, slot, count=1):
         return ref.at[pl.ds(pl.multiple_of(slot * 16, 16), 16 * count)]
 
-    def to_columns(src, dst, ss, rs):
-        def served(n):
-            return lax.rem(chip_x + n // 4, 4) * 8 + lax.rem(chip_z + 6 + lax.rem(n, 4), 8)
-
-        def body(n, carry):
-            c = served(n)
-            copy(both_fields(src, c), both_fields(dst, 8 + pair), ss, rs, up, c).start()
-            copy(both_fields(src, 32 + c), both_fields(dst, 40 + pair), ss, rs, down, c).start()
-            return carry
-
-        lax.fori_loop(0, 16, body, 0)
-
-        @pl.when(far)
-        def _():
-            def far_body(n, carry):
-                c = served(n)
-                copy(both_fields(src, 64 + c), both_fields(dst, far_slot), ss, rs, far_row, c).start()
+    def to_columns(src, dst, step, ss, rs):
+        near_by, opposite, second = shifts(step)
+
+        def send(variant, slot, row):
+            def body(n, carry):
+                c = lax.rem(chip_x + lax.rem(n, 4), 4) * 8 + lax.rem(chip_z + 6 + n // 4, 8)
+                copy(both_fields(src, 32 * variant + c), both_fields(dst, slot), ss, rs, row, c).start()
                 return carry
 
-            lax.fori_loop(0, 16, far_body, 0)
+            lax.fori_loop(0, 16, body, 0)
+
+        to_windows(src, 2, second)
+        pl.when(far)(lambda: send(2, far_slot, far_row))
+        to_windows(src, 0, near_by)
+        send(0, 8 + pair, up)
+        to_windows(src, 1, opposite)
+        send(1, 40 + pair, down)
 
     def columns_sent(src, ss, rs):
         all_tiles(src, 64, ss, rs).wait_send()
@@ -346,12 +339,10 @@
         ref[960:1024, :] = jnp.zeros((64, 128), jnp.float32)
     all_tiles(got, 31, ssem.at[0], rsem.at[0]).wait_recv()
     to_spread(got)
-    to_windows_of(sent, 0)
     pl.semaphore_wait(ready, 4)
-    to_columns(sent, window, ssem.at[3], rsem.at[3])
+    to_columns(sent, window, 0, ssem.at[3], rsem.at[3])
     pending.append(lambda: columns_sent(sent, ssem.at[3], rsem.at[3]))
-    to_windows_of(later, 1)
-    to_columns(later, ahead, ssem.at[4], rsem.at[4])
+    to_columns(later, ahead, 1, ssem.at[4], rsem.at[4])
     pending.append(lambda: columns_sent(later, ssem.at[4], rsem.at[4]))
     all_tiles(west, 16, ssem.at[1], rsem.at[1]).wait_recv()
     all_tiles(east, 16, ssem.at[2], rsem.at[2]).wait_recv()
@@ -384,8 +375,7 @@
     pending.append(all_tiles(own2, 16, ssem.at[7], rsem.at[7]).wait_send)
     all_tiles(got2, 31, ssem.at[5], rsem.at[5]).wait_recv()
     to_spread(got2)
-    to_windows_of(third, 1)
-    to_columns(third, window2, ssem.at[8], rsem.at[8])
+    to_columns(third, window2, 1, ssem.at[8], rsem.at[8])
     pending.append(lambda: columns_sent(third, ssem.at[8], rsem.at[8]))
     few(sums_row, 31, 0).wait_recv()
     sums_to_col(jnp.sum(sums_row[...], axis=0), part_row, sums_col, 1)
@@ -403,22 +393,43 @@
 
     u = moved(rows_of(ahead, 0), rows_of(window2, 0), rows_of(window2, 1), c1, c2)
     w, z, packed = solve(u, rows_of(ahead, 1))
-    sums_to_row(packed, part2, sums2_row, 2)
-    pending.append(few(sums2_row, 31, 2).wait_send)
-    few(sums2_row, 31, 2).wait_recv()
-    sums_to_col(jnp.sum(sums2_row[...], axis=0), part2_row, sums2_col, 3)
-    pending.append(few(sums2_col, 7, 3).wait_send)
-    few(sums2_col, 7, 3).wait_recv()
-    c1, c2 = coefficients(jnp.sum(sums2_col[...], axis=0))
-    put_rows(stage, 0, moved(u, w, z, c1, c2))
-    block = [stage[16 * (24 + p) : 16 * (24 + p) + 8, :] for p in range(16)]
-    flat_rows[...] = jnp.concatenate(block, axis=0)
-    flat = jnp.concatenate([flat_rows[pl.ds(k, 32, stride=4), :] for k in range(4)], axis=1)
+    part2[...] = packed
+    to_core = copy(part2, sums2_core, s2sem.at[2], r2sem.at[2], j + 1 - 2 * lax.rem(j, 2), i)
+    to_core.start()
+    pending.append(to_core.wait_send)
+    put_rows(stage, 0, u)
+    put_rows(window, 0, w)
+    put_rows(window, 1, z)
+    to_core.wait_recv()
+    total = packed + sums2_core[...]
+    part2_chip[...] = total
+    chip_y = j // 2
+    sums2[chip_y * NGX + i] = total
+
+    def to_chips(n, carry):
+        y, c = lax.rem(chip_y + n // NGX, 4), lax.rem(i + n, NGX)
+        copy(part2_chip, sums2.at[chip_y * NGX + i], s2sem.at[3], r2sem.at[3], 2 * y + lax.rem(j, 2), c).start()
+        return carry
+
+    lax.fori_loop(1, 128, to_chips, 0)
+    pending.append(few(sums2, 127, 3).wait_send)
+    for f, (ref, at_f) in enumerate(((stage, 0), (window, 0), (window, 1))):
+        for p in range(16):
+            at = 16 * (24 + p) + 8 * at_f
+            flat_rows[128 * f + 8 * p : 128 * f + 8 * p + 8, :] = ref[at : at + 8, :]
+    flat = jnp.concatenate([flat_rows[pl.ds(k, 96, stride=4), :] for k in range(4)], axis=1)
     rho = lax.broadcasted_iota(jnp.int32, (512, 256), 0)
     col = lanes((512, 256))
     c = col & 127
-    back = ((rho >> 7) == (c & 3)) & ((rho & 127) == (col >> 7) * 64 + 16 + (c >> 2))
-    flat = permuted(flat, jnp.where(back, 1.0, 0.0).astype(jnp.bfloat16))
+    same = ((rho >> 7) == (c & 3)) & ((rho & 63) == 16 + (c >> 2))
+    plane, of_plane = (rho >> 6) & 1, col >> 7
+    straight = jnp.where(same & (plane == of_plane), 1.0, 0.0).astype(jnp.bfloat16)
+    halves = jnp.where(same, jnp.where(plane + of_plane == 2, -0.5, 0.5), 0.0).astype(jnp.bfloat16)
+    u = permuted(flat[:32], straight)
+    wz = permuted(flat[32:], halves)
+    few(sums2, 127, 3).wait_recv()
+    c1, c2 = coefficients(jnp.sum(sums2[...], axis=0))
+    flat = u + c1 * wz[:32] + c2 * wz[32:]
     out[0] = flat[:, :128]
     out[1] = flat[:, 128:]
 
@@ -438,8 +449,8 @@
         out_specs=vmem,
         scratch_shapes=[
             tiles(16), tiles(32), tiles(64), tiles(16), tiles(16), tiles(192), tiles(192), tiles(192), tiles(128), tiles(128), tiles(128),
-            tiles(16), tiles(32), tiles(16), tiles(16), tiles(128), tiles(16),
-            line, line, lines(32), lines(8), line, line, lines(32), lines(8),
+            tiles(16), tiles(32), tiles(16), tiles(16), tiles(128), tiles(48),
+            line, line, lines(32), lines(8), line, line, line, lines(128),
             pltpu.SemaphoreType.DMA((9,)), pltpu.SemaphoreType.DMA((9,)),
             pltpu.SemaphoreType.DMA((4,)), pltpu.SemaphoreType.DMA((4,)), pltpu.SemaphoreType.REGULAR,
         ],

time: 61.7 us -> 59.3 us (0.961)
  Pallas kernels: 60.1 us -> 57.7 us
    pallas_call x1, Pallas kernels: 60.1 us -> 57.7 us  [local(): pl.pallas_call(kernel, out_shape=jax.ShapeDtypeStruct(phase.shape, f32),...]
where the time goes in v3:
time: 59.3 us; the launch traced here: 59.1 us
  Pallas kernels  57.7 us (97%)
  local copies, waits for them, and re-layouts  1.38 us (2%)
    pallas_call x1, Pallas kernels, local(): pl.pallas_call(kernel, out_shape=jax.ShapeDtypeStruct(phase.shape, f32),...  57.7 us
    unnamed x1, local copies, waits for them, and re-layouts  1.38 us

profile of v3, /device:TPU:1, one launch (start us, length us, event | category | flops | bytes accessed | tf_op | source)
XLA Modules:
  0.0 59.1 jit_solution(10551212863476187671)
XLA Ops:
  0.0 57.7 %shard_map.37 = f32[2,32,128]{2,1,0:T(8,128)} custom-call(s32[2,8]{1,0:T(2,128)} %offsets.1, f32[2,32,128]{2,1,0:T(8,128)} %phase.1, f32[2,32,128]{2,1,0:T(8,128)} %velocity.1), custom_call_target="tpu_custom_call" | custom-call | tf_op jit(solution)/shard_map/pallas_call | solution.py:445
  57.7 1.4 %copy.5 = f32[2,32,128]{2,1,0:T(8,128)} copy(f32[2,32,128]{2,1,0:T(8,128)} %shard_map.37) | data formatting | bytes 65536

commit v4 on v3

--- a/solution.py
+++ b/solution.py
@@ -157,7 +157,7 @@
 def kernel(
     offsets, phase, velocity, out,
     own, got, spread, west, east, sent, later, third, window, ahead, stage,
-    own2, got2, west2, east2, window2, flat_rows,
+    own2, got2, west2, east2, window2,
     part, part_row, sums_row, sums_col, part2, part2_chip, sums2_core, sums2,
     ssem, rsem, s2sem, r2sem, ready,
 ):
@@ -166,9 +166,10 @@
     pair = held_by(i)
     up, down = lax.rem(j + 1, NGY), lax.rem(j + NGY - 1, NGY)
     up2, down2 = lax.rem(j + 2, NGY), lax.rem(j + NGY - 2, NGY)
-    far = (pair < 4) | (pair >= 12)
-    far_row = jnp.where(pair < 4, down2, up2)
-    far_slot = jnp.where(pair < 4, 56 + pair, pair - 8)
+    first_half = pair < 8
+    far_row = jnp.where(first_half, down2, up2)
+    far_tile = jnp.where(first_half, 112 + 2 * pair, 2 * pair - 15)
+    far_from = jnp.where(first_half, 0, 1)
     near_west, near_east = lax.rem(i + NGX - 1, NGX), lax.rem(i + 1, NGX)
 
     def tile(ref, slot, count=1):
@@ -195,12 +196,21 @@
     def all_tiles(ref, count, ss, rs):
         return copy(ref.at[pl.ds(0, 8 * count)], ref.at[pl.ds(0, 8 * count)], ss, rs, j, near_east)
 
+    def by_row(first, second):
+        count = first.shape[0]
+        top = (lax.broadcasted_iota(jnp.int32, first.shape, 0) & 7) < 4
+        return (
+            jnp.where(top, first, pltpu.roll(second, 4, 0)),
+            jnp.where(top, pltpu.roll(first, count - 4, 0), second),
+        )
+
     def to_spread(src):
         here = src[...]
         following = jnp.concatenate([here[8:], here[:8]], axis=0)
         m = lanes((256, 128)) & 63
-        spread[0:256, :] = jnp.where(m < 32, here, lane_roll(following, 32))
-        spread[256:512, :] = jnp.where(m < 32, lane_roll(here, 96), following)
+        first = jnp.where(m < 32, here, lane_roll(following, 32))
+        second = jnp.where(m < 32, lane_roll(here, 96), following)
+        spread[0:256, :], spread[256:512, :] = by_row(first, second)
 
     def to_windows(dst, variant, shift):
         start = lax.rem(shift // 4 + (4096 - 16), 1024)
@@ -224,7 +234,7 @@
 
     def shifts(step):
         above, below = offsets[step, up], offsets[step, j]
-        second = jnp.where(pair < 4, below + offsets[step, down], -(above + offsets[step, up2]))
+        second = jnp.where(first_half, below + offsets[step, down], -(above + offsets[step, up2]))
         return -above, below, second
 
     def both_fields(ref, slot, count=1):
@@ -233,43 +243,51 @@
     def to_columns(src, dst, step, ss, rs):
         near_by, opposite, second = shifts(step)
 
+        def served(n):
+            return lax.rem(chip_x + lax.rem(n, 4), 4) * 8 + lax.rem(chip_z + 6 + n // 4, 8)
+
         def send(variant, slot, row):
             def body(n, carry):
-                c = lax.rem(chip_x + lax.rem(n, 4), 4) * 8 + lax.rem(chip_z + 6 + n // 4, 8)
+                c = served(n)
                 copy(both_fields(src, 32 * variant + c), both_fields(dst, slot), ss, rs, row, c).start()
                 return carry
 
             lax.fori_loop(0, 16, body, 0)
 
         to_windows(src, 2, second)
-        pl.when(far)(lambda: send(2, far_slot, far_row))
+
+        def far_body(n, carry):
+            c = served(n)
+            copy(tile(src, 2 * (64 + c) + far_from), tile(dst, far_tile), ss, rs, far_row, c).start()
+            return carry
+
+        lax.fori_loop(0, 16, far_body, 0)
         to_windows(src, 0, near_by)
         send(0, 8 + pair, up)
         to_windows(src, 1, opposite)
         send(1, 40 + pair, down)
 
     def columns_sent(src, ss, rs):
-        all_tiles(src, 64, ss, rs).wait_send()
-
-        @pl.when(far)
-        def _():
-            all_tiles(src, 32, ss, rs).wait_send()
+        all_tiles(src, 80, ss, rs).wait_send()
 
     def own_windows(centre, side_west, side_east, targets):
         m = lanes((128, 128)) & 63
-        for f, turns in enumerate(((112, 16, 48), (80, 112, 16))):
-            whole = jnp.where(
+        fields = (
+            jnp.where(
                 m < 16,
                 lane_roll(side_west[...], turns[0]),
                 jnp.where(m < 48, lane_roll(centre[...], turns[1]), lane_roll(side_east[...], turns[2])),
             )
+            for turns in ((112, 16, 48), (80, 112, 16))
+        )
+        for h, whole in enumerate(by_row(*fields)):
             for target in targets:
                 for p in range(16):
-                    at = 16 * (24 + p) + 8 * f
+                    at = 16 * (24 + p) + 8 * h
                     target[at : at + 8, :] = whole[8 * p : 8 * p + 8]
 
     def row_at(f, r, k):
-        return pl.ds(16 * (r // 2) + 8 * f + 4 * (r % 2) + k, 8, stride=128)
+        return pl.ds(16 * (r % 8) + 8 * (r // 8) + 4 * f + k, 8, stride=128)
 
     def rows_of(ref, f):
         return [jnp.stack([ref[row_at(f, r, k), :] for k in range(4)]) for r in range(16)]
@@ -324,7 +342,9 @@
     for k in range(4):
         u, v = (split[64 * f : 64 * f + 64, 128 * k : 128 * k + 128] for f in range(2))
         u, v = (cut[:32] + lane_roll(cut[32:], 64) for cut in (u, v))
-        own[pl.ds(k, 32, stride=4), :] = u + lane_roll(v, 32)
+        u = u + lane_roll(v, 32)
+        for g in range(4):
+            own[pl.ds(64 * (g // 2) + 4 * (g % 2) + k, 8, stride=8), :] = u[8 * g : 8 * g + 8]
 
     pl.semaphore_wait(barrier, NGX - 1 + NGY - 1)
     to_row(own, got, ssem.at[0], rsem.at[0])
@@ -335,8 +355,9 @@
     pending.append(all_tiles(own, 16, ssem.at[1], rsem.at[1]).wait_send)
     pending.append(all_tiles(own, 16, ssem.at[2], rsem.at[2]).wait_send)
     for ref in (window, ahead, window2):
-        ref[0:64, :] = jnp.zeros((64, 128), jnp.float32)
-        ref[960:1024, :] = jnp.zeros((64, 128), jnp.float32)
+        for p in range(8):
+            for at in (16 * p, 16 * (56 + p) + 8):
+                ref[at : at + 8, :] = jnp.zeros((8, 128), jnp.float32)
     all_tiles(got, 31, ssem.at[0], rsem.at[0]).wait_recv()
     to_spread(got)
     pl.semaphore_wait(ready, 4)
@@ -363,9 +384,8 @@
     m = lanes() & 63
     for p in range(16):
         at = 16 * (24 + p)
-        own2[8 * p : 8 * p + 8, :] = jnp.where(
-            m < 32, lane_roll(stage[at : at + 8, :], 112), lane_roll(stage[at + 8 : at + 16, :], 16)
-        )
+        first, second = by_row(stage[at : at + 8, :], stage[at + 8 : at + 16, :])
+        own2[8 * p : 8 * p + 8, :] = jnp.where(m < 32, lane_roll(first, 112), lane_roll(second, 16))
     to_row(own2, got2, ssem.at[5], rsem.at[5])
     pending.append(all_tiles(got2, 31, ssem.at[5], rsem.at[5]).wait_send)
     sums_to_row(packed, part, sums_row, 0)
@@ -413,11 +433,20 @@
 
     lax.fori_loop(1, 128, to_chips, 0)
     pending.append(few(sums2, 127, 3).wait_send)
-    for f, (ref, at_f) in enumerate(((stage, 0), (window, 0), (window, 1))):
-        for p in range(16):
-            at = 16 * (24 + p) + 8 * at_f
-            flat_rows[128 * f + 8 * p : 128 * f + 8 * p + 8, :] = ref[at : at + 8, :]
-    flat = jnp.concatenate([flat_rows[pl.ds(k, 96, stride=4), :] for k in range(4)], axis=1)
+    flat = jnp.concatenate(
+        [
+            jnp.concatenate(
+                [
+                    ref[pl.ds(16 * (24 + 8 * (g // 2)) + 8 * (g % 2) + 4 * f + k, 8, stride=16), :]
+                    for ref, f in ((stage, 0), (window, 0), (window, 1))
+                    for g in range(4)
+                ],
+                axis=0,
+            )
+            for k in range(4)
+        ],
+        axis=1,
+    )
     rho = lax.broadcasted_iota(jnp.int32, (512, 256), 0)
     col = lanes((512, 256))
     c = col & 127
@@ -449,7 +478,7 @@
         out_specs=vmem,
         scratch_shapes=[
             tiles(16), tiles(32), tiles(64), tiles(16), tiles(16), tiles(192), tiles(192), tiles(192), tiles(128), tiles(128), tiles(128),
-            tiles(16), tiles(32), tiles(16), tiles(16), tiles(128), tiles(48),
+            tiles(16), tiles(32), tiles(16), tiles(16), tiles(128),
             line, line, lines(32), lines(8), line, line, line, lines(128),
             pltpu.SemaphoreType.DMA((9,)), pltpu.SemaphoreType.DMA((9,)),
             pltpu.SemaphoreType.DMA((4,)), pltpu.SemaphoreType.DMA((4,)), pltpu.SemaphoreType.REGULAR,

time: 59.3 us -> 57.8 us (0.975)
  Pallas kernels: 57.7 us -> 56.2 us
    pallas_call x1, Pallas kernels: 57.7 us -> 56.2 us  [local(): pl.pallas_call(kernel, out_shape=jax.ShapeDtypeStruct(phase.shape, f32),...]
where the time goes in v4:
time: 57.8 us; the launch traced here: 57.6 us
  Pallas kernels  56.2 us (97%)
  local copies, waits for them, and re-layouts  1.38 us (2%)
    pallas_call x1, Pallas kernels, local(): pl.pallas_call(kernel, out_shape=jax.ShapeDtypeStruct(phase.shape, f32),...  56.2 us
    unnamed x1, local copies, waits for them, and re-layouts  1.38 us

profile of v4, /device:TPU:1, one launch (start us, length us, event | category | flops | bytes accessed | tf_op | source)
XLA Modules:
  0.0 57.6 jit_solution(8318164009832975233)
XLA Ops:
  0.0 56.2 %shard_map.37 = f32[2,32,128]{2,1,0:T(8,128)} custom-call(s32[2,8]{1,0:T(2,128)} %offsets.1, f32[2,32,128]{2,1,0:T(8,128)} %phase.1, f32[2,32,128]{2,1,0:T(8,128)} %velocity.1), custom_call_target="tpu_custom_call" | custom-call | tf_op jit(solution)/shard_map/pallas_call | solution.py:474
  56.2 1.4 %copy.5 = f32[2,32,128]{2,1,0:T(8,128)} copy(f32[2,32,128]{2,1,0:T(8,128)} %shard_map.37) | data formatting | bytes 65536

commit v5 on v4

--- a/solution.py
+++ b/solution.py
@@ -212,13 +212,13 @@
         second = jnp.where(m < 32, lane_roll(here, 96), following)
         spread[0:256, :], spread[256:512, :] = by_row(first, second)
 
-    def to_windows(dst, variant, shift):
+    def to_windows(dst, variant, shift, parts=(0, 256)):
         start = lax.rem(shift // 4 + (4096 - 16), 1024)
         block, g = start // 32, lax.rem(start, 32)
         whole = jnp.full((8, 128), block, jnp.int32)
         m = lanes((256, 128)) & 63
-        for f in range(2):
-            near = spread[256 * f : 256 * f + 256, :].reshape(32, 8, 128)
+        for h, part_at in enumerate(parts):
+            near = spread[pl.ds(part_at, 256), :].reshape(32, 8, 128)
             for bit in range(5):
                 step = 1 << bit
                 ahead_of = jnp.concatenate([near[step:], near[:step]], axis=0)
@@ -229,7 +229,7 @@
                 m + g < 64, lane_roll(near, lax.rem(128 - g, 128)), lane_roll(next_, 64 - g)
             )
             for c in range(NGX):
-                at = 16 * (32 * variant + c) + 8 * f
+                at = 16 * (32 * variant + c) + 8 * h
                 dst[at : at + 8, :] = moved_on[8 * c : 8 * c + 8]
 
     def shifts(step):
@@ -254,11 +254,11 @@
 
             lax.fori_loop(0, 16, body, 0)
 
-        to_windows(src, 2, second)
+        to_windows(src, 2, second, (pl.multiple_of(far_from * 256, 256),))
 
         def far_body(n, carry):
             c = served(n)
-            copy(tile(src, 2 * (64 + c) + far_from), tile(dst, far_tile), ss, rs, far_row, c).start()
+            copy(tile(src, 2 * (64 + c)), tile(dst, far_tile), ss, rs, far_row, c).start()
             return carry
 
         lax.fori_loop(0, 16, far_body, 0)
@@ -375,10 +375,12 @@
         w = precondition(r)
         q = operate(w)
         z = precondition(q)
-        y = operate(z)
-        return w, z, packed_sums(((r, w), (w, q), (r, z), (q, z), (z, y)))
-
-    w, z, packed = solve(rows_of(window, 0), rows_of(window, 1))
+        return r, w, q, z
+
+    def sums_of(r, w, q, z):
+        return packed_sums(((r, w), (w, q), (r, z), (q, z), (z, operate(z))))
+
+    r, w, q, z = solve(rows_of(window, 0), rows_of(window, 1))
     put_rows(stage, 0, w)
     put_rows(stage, 1, z)
     m = lanes() & 63
@@ -388,7 +390,7 @@
         own2[8 * p : 8 * p + 8, :] = jnp.where(m < 32, lane_roll(first, 112), lane_roll(second, 16))
     to_row(own2, got2, ssem.at[5], rsem.at[5])
     pending.append(all_tiles(got2, 31, ssem.at[5], rsem.at[5]).wait_send)
-    sums_to_row(packed, part, sums_row, 0)
+    sums_to_row(sums_of(r, w, q, z), part, sums_row, 0)
     pending.append(few(sums_row, 31, 0).wait_send)
     to_sides(own2, west2, east2, 6)
     pending.append(all_tiles(own2, 16, ssem.at[6], rsem.at[6]).wait_send)
@@ -412,7 +414,8 @@
         return [a + 0.5 * mixed(c1 * b + c2 * d) for a, b, d in zip(u, w, z)]
 
     u = moved(rows_of(ahead, 0), rows_of(window2, 0), rows_of(window2, 1), c1, c2)
-    w, z, packed = solve(u, rows_of(ahead, 1))
+    r, w, q, z = solve(u, rows_of(ahead, 1))
+    packed = sums_of(r, w, q, z)
     part2[...] = packed
     to_core = copy(part2, sums2_core, s2sem.at[2], r2sem.at[2], j + 1 - 2 * lax.rem(j, 2), i)
     to_core.start()

time: 57.8 us -> 57.5 us (level)
  no operation moved by 1% of the time
where the time goes in v5:
time: 57.5 us; the launch traced here: 57.3 us
  Pallas kernels  55.9 us (97%)
  local copies, waits for them, and re-layouts  1.38 us (2%)
    pallas_call x1, Pallas kernels, local(): pl.pallas_call(kernel, out_shape=jax.ShapeDtypeStruct(phase.shape, f32),...  55.9 us
    unnamed x1, local copies, waits for them, and re-layouts  1.38 us

profile of v5, /device:TPU:1, one launch (start us, length us, event | category | flops | bytes accessed | tf_op | source)
XLA Modules:
  0.0 57.3 jit_solution(10102115720934821751)
XLA Ops:
  0.0 55.9 %shard_map.37 = f32[2,32,128]{2,1,0:T(8,128)} custom-call(s32[2,8]{1,0:T(2,128)} %offsets.1, f32[2,32,128]{2,1,0:T(8,128)} %phase.1, f32[2,32,128]{2,1,0:T(8,128)} %velocity.1), custom_call_target="tpu_custom_call" | custom-call | tf_op jit(solution)/shard_map/pallas_call | solution.py:477
  55.9 1.4 %copy.5 = f32[2,32,128]{2,1,0:T(8,128)} copy(f32[2,32,128]{2,1,0:T(8,128)} %shard_map.37) | data formatting | bytes 65536
